TPU v7x, 32 devices: a whole 2x2x4 slice. The times are simulated.
32 devices in a mesh: groups: 2 (over y), seq: 4 (over z), segment: 2 (over x), owner: 2 (over core).
Axes of the slice: x: 2, y: 2, z: 4, core: 2. Of those that a mesh axis runs over, the one named last changes fastest.
Arguments:
- layer_input_rows: bfloat16 [2, 512, 5376], P('segment', ('groups', 'seq')), parts along dimension 1, may hold values from -40 to 40
- encoded_query_rows: bfloat16 [2, 512, 2048], P('segment', ('groups', 'seq'), 'owner'), parts along dimension 1, may hold values from -213 to 213
- encoded_key_rows: bfloat16 [2, 512, 1024], P('segment', ('groups', 'seq'), 'owner'), parts along dimension 1, may hold values from -6 to 6
- layer_norm_gain: float32 [2, 5376], P('segment'), may hold values from 0.25 to 1.75
- base_value_matrix: bfloat16 [2, 5376, 1024], P('segment', ('seq', 'owner')), may hold values from -0.078125 to 0.078125
- adapter_down_panels: bfloat16 [2, 8, 5376, 64], P('segment', 'seq', 'owner'), may hold values from -0.078125 to 0.078125
- adapter_up_panels: bfloat16 [2, 8, 64, 1024], P('segment', 'seq', None, 'owner'), may hold values from -0.75 to 0.75
- request_token_lengths: int32 [8], P('groups'), parts along dimension 0, may hold values from 1 to 128, 256 in all
- adapter_per_request: int32 [8], P('groups'), parts along dimension 0, may hold values from 0 to 7
- rank_per_adapter: int32 [8], replicated, may hold values from 16 to 64
- slot_per_adapter: int32 [8], replicated, may hold values from 0 to 7, each once
Outputs:
- layer_output: bfloat16 [2, 512, 2048], P('segment', ('groups', 'seq'), 'owner'), parts along dimension 1
There are 2 independent parts, one for each index of `groups`. A program takes and returns all parts, laid end to end along the dimension named above; an argument that names none is the same for every part. Nothing has to cross between parts.
All inputs are finite; a program needn't handle non-finite values.
Results may differ from a plain program's by a relative error of at most 0.0065.
Values may be sent and summed in bfloat16 or wider, within the bound.
A program may use at most 128 MiB of HBM per device.

v0:
```python
import jax
import jax.numpy as jnp
from jax import lax
from jax.sharding import PartitionSpec as P

WINDOW = 1024
HEADS = 16
KEY_VALUE_HEADS = 8
HEAD_SIZE = 128


query_scale = 168.0 ** (-0.5)
adapter_strength = 32.0
norm_eps = 1e-06


def broadcast(x, axis, root):
    mine = lax.axis_index(axis) == root
    return lax.psum(jnp.where(mine, x, jnp.zeros_like(x)), axis)


def from_behind(value, axis, steps):
    count = lax.axis_size(axis)
    first, last = (max(0, -steps), min(count, count - steps))
    return lax.ppermute(value, axis, [(source, source + steps) for source in range(first, last)])


def per_device(
    layer_input_rows,
    encoded_query_rows,
    encoded_key_rows,
    layer_norm_gain,
    base_value_matrix,
    adapter_down_panels,
    adapter_up_panels,
    request_token_lengths,
    adapter_per_request,
    rank_per_adapter,
    slot_per_adapter,
):
    hidden = layer_input_rows[0]
    row_count = hidden.shape[0]
    seq_now = lax.axis_index("seq")
    owner_now = lax.axis_index("owner")
    reach_count = min(WINDOW // row_count, lax.axis_size("seq") - 1)
    requests = request_token_lengths.shape[0]
    library = slot_per_adapter.shape[0]
    slots_here = adapter_down_panels.shape[1]
    rows_halved = adapter_down_panels.shape[2]
    rank_span_width = adapter_down_panels.shape[3]
    key_value_halved = adapter_up_panels.shape[3]
    group_size = HEADS // KEY_VALUE_HEADS
    request_ends = jnp.cumsum(request_token_lengths)
    position = seq_now * row_count + jnp.arange(row_count, dtype=jnp.int32)
    context = seq_now * row_count + jnp.arange(-reach_count * row_count, row_count, dtype=jnp.int32)
    request_lookup = jnp.sum((position[:, None] >= request_ends[None, :]).astype(jnp.int32), axis=1)
    request_ctx = jnp.sum((context[:, None] >= request_ends[None, :]).astype(jnp.int32), axis=1)
    live_mask = (context[None, :] <= position[:, None]) & (
        context[None, :] > position[:, None] - WINDOW
    )
    live_mask = (
        live_mask & (context[None, :] >= 0) & (request_ctx[None, :] == request_lookup[:, None])
    )
    choose = adapter_per_request[:, None] == jnp.arange(library, dtype=jnp.int32)[None, :]
    slot_of = jnp.sum(jnp.where(choose, slot_per_adapter[None, :], 0), axis=1)
    rank_lookup = jnp.sum(jnp.where(choose, rank_per_adapter[None, :], 0), axis=1)
    scale_lookup = adapter_strength / rank_lookup.astype(jnp.float32)
    in_request = request_lookup[:, None] == jnp.arange(requests, dtype=jnp.int32)[None, :]
    column_live = jnp.arange(rank_span_width, dtype=jnp.int32)[None, :] < rank_lookup[:, None]
    row_gain_weight = jnp.where(in_request, scale_lookup[None, :], jnp.float32(0.0))
    down_panel_here = adapter_down_panels[0]
    up_panel_here = adapter_up_panels[0]
    queries = encoded_query_rows[0]
    keys_own = encoded_key_rows[0]
    key_heads = keys_own.shape[1] // HEAD_SIZE
    wide_rows = hidden.astype(jnp.float32)
    normalized_rows = wide_rows * lax.rsqrt(
        jnp.mean(wide_rows * wide_rows, axis=1, keepdims=True) + norm_eps
    )
    normalized_rows = (normalized_rows * layer_norm_gain[0][None, :]).astype(jnp.bfloat16)
    normed_half = lax.dynamic_slice_in_dim(normalized_rows, owner_now * rows_halved, rows_halved, 1)
    full_value = jnp.dot(
        normalized_rows,
        lax.all_gather(base_value_matrix[0], ("seq", "owner"), axis=0, tiled=True),
        preferred_element_type=jnp.float32,
    )
    value_base_rows = lax.dynamic_slice_in_dim(
        full_value, owner_now * key_value_halved, key_value_halved, 1
    )

    def fetch_one(reduced_rows, request_index):
        owner_slot = slot_of[request_index]
        holder = owner_slot // slots_here
        local_slot = owner_slot % slots_here
        down_local = lax.dynamic_slice_in_dim(down_panel_here, local_slot, 1, 0)
        up_local = lax.dynamic_slice_in_dim(up_panel_here, local_slot, 1, 0)
        down_piece, up_piece = (
            broadcast(down_local, "seq", holder),
            broadcast(up_local, "seq", holder),
        )
        keep_mask = in_request[:, request_index][:, None] & column_live[request_index][None, :]
        matrix_product = jnp.dot(normed_half, down_piece[0], preferred_element_type=jnp.float32)
        return (reduced_rows + jnp.where(keep_mask, matrix_product, jnp.float32(0.0)), up_piece[0])

    start_low = jnp.zeros((row_count, rank_span_width), jnp.float32)
    reduced_rows, panels_up = lax.scan(fetch_one, start_low, jnp.arange(requests, dtype=jnp.int32))
    reduced_rows = lax.psum(reduced_rows, "owner").astype(jnp.bfloat16)
    raised_rows = jnp.einsum(
        "tr,qrk->qtk", reduced_rows, panels_up, preferred_element_type=jnp.float32
    )
    adapter_value = jnp.sum(row_gain_weight.T[:, :, None] * raised_rows, axis=0)
    value_output_rows = (value_base_rows + adapter_value).astype(jnp.bfloat16)
    key_parts = []
    value_parts = []
    for shift_by in range(reach_count, 0, -1):
        key_piece, value_piece = from_behind((keys_own, value_output_rows), "seq", shift_by)
        key_parts.append(key_piece)
        value_parts.append(value_piece)
    keys_all = jnp.concatenate(key_parts + [keys_own], axis=0)
    values_all = jnp.concatenate(value_parts + [value_output_rows], axis=0)
    query_view = queries.reshape(row_count, key_heads, group_size, HEAD_SIZE)
    key_view = keys_all.reshape(-1, key_heads, HEAD_SIZE)
    value_view = values_all.reshape(-1, key_heads, HEAD_SIZE)
    head_outputs = []
    for head_index in range(key_heads):
        query_head = query_view[:, head_index]
        scores = (
            jnp.einsum(
                "tcd,jd->ctj",
                query_head,
                key_view[:, head_index],
                preferred_element_type=jnp.float32,
            )
            * query_scale
        )
        scores = jnp.where(live_mask[None], scores, jnp.float32(-1e30))
        row_max = jnp.max(scores, axis=-1, keepdims=True)
        weights = jnp.exp(scores - row_max)
        row_total = jnp.sum(weights, axis=-1, keepdims=True)
        softmax_rows = (weights / row_total).astype(jnp.bfloat16)
        mixed = jnp.einsum(
            "ctj,jd->tcd",
            softmax_rows,
            value_view[:, head_index],
            preferred_element_type=jnp.float32,
        )
        head_outputs.append(mixed.astype(jnp.bfloat16).reshape(row_count, group_size * HEAD_SIZE))
    result = jnp.concatenate(head_outputs, axis=1)
    return result[None]


def solution(mesh):
    in_specs = (
        P("segment", ("groups", "seq"), None),
        P("segment", ("groups", "seq"), "owner"),
        P("segment", ("groups", "seq"), "owner"),
        P("segment", None),
        P("segment", ("seq", "owner"), None),
        P("segment", "seq", "owner", None),
        P("segment", "seq", None, "owner"),
        P("groups"),
        P("groups"),
        P(),
        P(),
    )
    out_specs = P("segment", ("groups", "seq"), "owner")
    return jax.shard_map(
        per_device, mesh=mesh, in_specs=in_specs, out_specs=out_specs, check_vma=False
    )
```

profile of v0, /device:TPU:0, one launch (start us, length us, event | category | flops | bytes accessed | tf_op | source)
XLA Modules:
  0.0 353.9 jit_solution(13641821148216391470)
XLA Ops:
  7.4 1.4 fusion.8
  10.7 1.7 copy.36
  13.4 211.6 %while.15 = (s32[]{:T(128)}, f32[64,64]{0,1:T(8,128)S(1)}, bf16[4,64,512]{2,1,0:T(8,128)(2,1)S(1)}, s32[4]{0:T(128)S(1)}, pred[64,4]{0,1:T(4,128)(4,1)S(1)}, /*i...) while((s32[]{:T(128)}, f32[64,64]{0,1:T(8,128)S(1)}, ...), condition=%wide.region_8.9_spmd.clone, body=%wide.region_5.8_spmd.clone.sunk | while | flops 22446112 | bytes 4817837 | solution.py:106
  19.1 0.9 select_bitcast_fusion.2
  20.7 45.7 %all-reduce.5.cloned.1.call-done = (bf16[2688,64]{1,0:T(8,128)(2,1)}, bf16[1,64,512]{2,1,0:T(8,128)(2,1)}) async-done(((bf16[2688,64]{1,0:T(8,128)(2,1)}, bf16[1,64,512]{2,1,0:T(8,128)(2,1)}), (bf16[2688,64]{1,0:T(8,128)(2,1)}, bf16[1,64,512]{2,1,0:T(8,128)(2,1)})) %all-reduce.5.cloned.1.call-update) | async-done | bytes 409616 | tf_op jit(solution)/shard_map/while/body/eval_jaxpr/psum | solution.py:19
  67.2 1.5 fusion.74
  74.5 0.9 select_bitcast_fusion.2
  76.1 42.3 %all-reduce.5.cloned.1.call-done = (bf16[2688,64]{1,0:T(8,128)(2,1)}, bf16[1,64,512]{2,1,0:T(8,128)(2,1)}) async-done(((bf16[2688,64]{1,0:T(8,128)(2,1)}, bf16[1,64,512]{2,1,0:T(8,128)(2,1)}), (bf16[2688,64]{1,0:T(8,128)(2,1)}, bf16[1,64,512]{2,1,0:T(8,128)(2,1)})) %all-reduce.5.cloned.1.call-update) | async-done | bytes 409616 | tf_op jit(solution)/shard_map/while/body/eval_jaxpr/psum | solution.py:19
  119.3 1.5 fusion.74
  126.6 0.9 select_bitcast_fusion.2
  128.2 42.3 %all-reduce.5.cloned.1.call-done = (bf16[2688,64]{1,0:T(8,128)(2,1)}, bf16[1,64,512]{2,1,0:T(8,128)(2,1)}) async-done(((bf16[2688,64]{1,0:T(8,128)(2,1)}, bf16[1,64,512]{2,1,0:T(8,128)(2,1)}), (bf16[2688,64]{1,0:T(8,128)(2,1)}, bf16[1,64,512]{2,1,0:T(8,128)(2,1)})) %all-reduce.5.cloned.1.call-update) | async-done | bytes 409616 | tf_op jit(solution)/shard_map/while/body/eval_jaxpr/psum | solution.py:19
  171.4 1.5 fusion.74
  180.3 42.3 %all-reduce.5.cloned.1.call-done = (bf16[2688,64]{1,0:T(8,128)(2,1)}, bf16[1,64,512]{2,1,0:T(8,128)(2,1)}) async-done(((bf16[2688,64]{1,0:T(8,128)(2,1)}, bf16[1,64,512]{2,1,0:T(8,128)(2,1)}), (bf16[2688,64]{1,0:T(8,128)(2,1)}, bf16[1,64,512]{2,1,0:T(8,128)(2,1)})) %all-reduce.5.cloned.1.call-update) | async-done | bytes 409616 | tf_op jit(solution)/shard_map/while/body/eval_jaxpr/psum | solution.py:19
  223.4 1.5 fusion.74
  225.8 3.7 %collective-permute-start.3 = (bf16[64,512]{1,0:T(8,128)(2,1)S(1)}, bf16[64,512]{1,0:T(8,128)(2,1)S(1)}, u32[]{:S(2)}, u32[]{:S(2)}) collective-permute-start(bf16[64,512]{1,0:T(8,128)(2,1)S(1)} %bitcast.212), channel_id=1, source_target_pairs={{0,12},{1,13},{2,14},{3,15},{16,28},{17,29},{18,30},{19,31}} | collective-permute-start | bytes 196616 | tf_op jit(solution)/shard_map/ppermute | solution.py:25
  229.5 1.3 collective-permute-start.4
  230.8 2.5 collective-permute-start.5
  233.5 3.4 psum.27
  239.3 90.8 %all-gather.3.cloned.1.call-done = bf16[1,5376,1024]{2,1,0:T(8,128)(2,1)} async-done(((bf16[1,672,1024]{2,1,0:T(8,128)(2,1)}), bf16[1,5376,1024]{2,1,0:T(8,128)(2,1)}) %all-gather.3.cloned.1.call-update) | async-done | bytes 11010064 | tf_op jit(solution)/shard_map/all_gather | solution.py:84
  330.1 6.1 %fusion.6 = f32[64,1024]{1,0:T(8,128)S(1)} fusion(bf16[64,5376]{1,0:T(8,128)(2,1)S(1)} %fusion.10, bf16[1,5376,1024]{2,1,0:T(8,128)(2,1)} %all-gather.3.cloned.1.call-done), kind=kOutput, calls=%fused_computation.12 | convolution fusion | flops 704643072 | bytes 11960320 | tf_op jit(solution)/shard_map/dot_general | solution.py:82
  336.3 2.3 collective-permute-start
  338.6 1.3 collective-permute-start.1
  339.9 2.5 collective-permute-start.2
  342.7 1.5 collective-permute-done.2
  (99 shorter events, 20.7 us)
Async XLA Ops:
  7.4 5.1 %copy-start.4 = (f32[1,5376]{1,0:T(1,128)S(1)}, f32[1,5376]{1,0:T(1,128)}, u32[]{:S(2)}) copy-start(f32[1,5376]{1,0:T(1,128)} %param.16) | copy-start | bytes 64516
  7.4 5.2 %copy-start = (bf16[1,64,5376]{2,1,0:T(8,128)(2,1)S(1)}, bf16[1,64,5376]{2,1,0:T(8,128)(2,1)}, u32[]{:S(2)}) copy-start(bf16[1,64,5376]{2,1,0:T(8,128)(2,1)} %param.13) | copy-start | bytes 2064388
  12.5 0.9 copy-start.1
  13.4 53.0 %all-reduce.5.cloned.1.call-start = ((), (), s32[]{:S(2)}) async-start(), calls=%async_computation.1 | async-start | bytes 1507328 | tf_op jit(solution)/shard_map/while/body/eval_jaxpr/psum | solution.py:19
  68.7 49.7 %all-reduce.5.cloned.1.call-start = ((), (), s32[]{:S(2)}) async-start(), calls=%async_computation.1 | async-start | bytes 1507328 | tf_op jit(solution)/shard_map/while/body/eval_jaxpr/psum | solution.py:19
  120.8 49.7 %all-reduce.5.cloned.1.call-start = ((), (), s32[]{:S(2)}) async-start(), calls=%async_computation.1 | async-start | bytes 1507328 | tf_op jit(solution)/shard_map/while/body/eval_jaxpr/psum | solution.py:19
  172.9 49.7 %all-reduce.5.cloned.1.call-start = ((), (), s32[]{:S(2)}) async-start(), calls=%async_computation.1 | async-start | bytes 1507328 | tf_op jit(solution)/shard_map/while/body/eval_jaxpr/psum | solution.py:19
  224.9 0.8 copy-start.3
  225.0 8.4 %copy-start.2 = (bf16[1,64,1024]{2,1,0:T(8,128)(2,1)S(1)}, bf16[1,64,1024]{2,1,0:T(8,128)(2,1)}, u32[]{:S(2)}) copy-start(bf16[1,64,1024]{2,1,0:T(8,128)(2,1)} %param.14) | copy-start | bytes 393220
  225.0 105.1 %all-gather.3.cloned.1.call-start = ((), (), s32[]{:S(2)}) async-start(), calls=%async_computation | async-start | bytes 12386304 | tf_op jit(solution)/shard_map/all_gather | solution.py:84
  225.8 11.7 %collective-permute-start.3 = (bf16[64,512]{1,0:T(8,128)(2,1)S(1)}, bf16[64,512]{1,0:T(8,128)(2,1)S(1)}, u32[]{:S(2)}, u32[]{:S(2)}) collective-permute-start(bf16[64,512]{1,0:T(8,128)(2,1)S(1)} %bitcast.212), channel_id=1, source_target_pairs={{0,12},{1,13},{2,14},{3,15},{16,28},{17,29},{18,30},{19,31}} | collective-permute-start | bytes 196616 | tf_op jit(solution)/shard_map/ppermute | solution.py:25
  229.5 8.0 %collective-permute-start.4 = (bf16[64,512]{1,0:T(8,128)(2,1)S(1)}, bf16[64,512]{1,0:T(8,128)(2,1)S(1)}, u32[]{:S(2)}, u32[]{:S(2)}) collective-permute-start(bf16[64,512]{1,0:T(8,128)(2,1)S(1)} %bitcast.213), channel_id=1, source_target_pairs={{0,8},{4,12},{1,9},{5,13},{2,10},{6,14},{3,11},{7,15},{16,24},{20,... | collective-permute-start | bytes 196616 | tf_op jit(solution)/shard_map/ppermute | solution.py:25
  230.8 6.8 %collective-permute-start.5 = (bf16[64,512]{1,0:T(8,128)(2,1)S(1)}, bf16[64,512]{1,0:T(8,128)(2,1)S(1)}, u32[]{:S(2)}, u32[]{:S(2)}) collective-permute-start(bf16[64,512]{1,0:T(8,128)(2,1)S(1)} %bitcast.214), channel_id=1, source_target_pairs={{0,4},{4,8},{8,12},{1,5},{5,9},{9,13},{2,6},{6,10},{10,14},{3,7},{... | collective-permute-start | bytes 196616 | tf_op jit(solution)/shard_map/ppermute | solution.py:25
  336.3 6.4 %collective-permute-start = (bf16[64,512]{1,0:T(8,128)(2,1)S(1)}, bf16[64,512]{1,0:T(8,128)(2,1)S(1)}, u32[]{:S(2)}, u32[]{:S(2)}) collective-permute-start(bf16[64,512]{1,0:T(8,128)(2,1)S(1)} %fusion.32), channel_id=1, source_target_pairs={{0,12},{1,13},{2,14},{3,15},{16,28},{17,29},{18,30},{19,31}} | collective-permute-start | bytes 196616 | tf_op jit(solution)/shard_map/ppermute | solution.py:25
  338.6 4.1 %collective-permute-start.1 = (bf16[64,512]{1,0:T(8,128)(2,1)S(1)}, bf16[64,512]{1,0:T(8,128)(2,1)S(1)}, u32[]{:S(2)}, u32[]{:S(2)}) collective-permute-start(bf16[64,512]{1,0:T(8,128)(2,1)S(1)} %fusion.32), channel_id=1, source_target_pairs={{0,8},{4,12},{1,9},{5,13},{2,10},{6,14},{3,11},{7,15},{16,24},{20,... | collective-permute-start | bytes 196616 | tf_op jit(solution)/shard_map/ppermute | solution.py:25
  339.9 4.4 %collective-permute-start.2 = (bf16[64,512]{1,0:T(8,128)(2,1)S(1)}, bf16[64,512]{1,0:T(8,128)(2,1)S(1)}, u32[]{:S(2)}, u32[]{:S(2)}) collective-permute-start(bf16[64,512]{1,0:T(8,128)(2,1)S(1)} %fusion.32), channel_id=1, source_target_pairs={{0,4},{4,8},{8,12},{1,5},{5,9},{9,13},{2,6},{6,10},{10,14},{3,7},{... | collective-permute-start | bytes 196616 | tf_op jit(solution)/shard_map/ppermute | solution.py:25
Sparse Core Ops, SparseCore 0:
  20.8 45.5 all-reduce.4
  76.2 42.1 all-reduce.4
  128.3 42.1 all-reduce.4
  180.4 42.1 all-reduce.4
Sparse Core Ops, SparseCore 1:
  227.1 103.0 all-gather.2
where the time goes:
time: 355 us; the launch traced here: 354 us
  waiting for transfers between devices  266 us (75%)
  loops' own time  18.5 us (5%)
  matrix products  15.6 us (4%)
  between operations  14.9 us (4%)
  starting transfers between devices  13.7 us (4%)
  local copies, waits for them, and re-layouts  11.6 us (3%)
  other arithmetic  10.8 us (3%)
    psum x4, waiting for transfers between devices, broadcast(): return lax.psum(jnp.where(mine, x, jnp.zeros_like(x)), axis)  173 us
    all_gather x1, waiting for transfers between devices, per_device(): lax.all_gather(base_value_matrix[0], ('seq', 'owner'), axis=0, tiled=True)  90.8 us
    another operation x1, loops' own time, per_device(): lax.scan(fetch_one, start_low, jnp.arange(requests, dtype=jnp.int32))  18.5 us
    ppermute x6, starting transfers between devices, from_behind(): lax.ppermute(value, axis, [(source, source + steps) for source in range(f...  13.5 us
  transfers between devices with their start and end apart: 11, of which 6 were waited for; matrix products, arithmetic and copies ran while one was open for 1% of the time, Pallas kernels for 0%

commit v1 on v0

--- a/solution.py
+++ b/solution.py
@@ -1,6 +1,10 @@
+import functools
+
 import jax
 import jax.numpy as jnp
 from jax import lax
+from jax.experimental import pallas as pl
+from jax.experimental.pallas import tpu as pltpu
 from jax.sharding import PartitionSpec as P
 
 WINDOW = 1024
@@ -149,6 +153,453 @@
     return result[None]
 
 
+ROWS, LANES = 16, 128
+
+
+def kernel(
+    n,
+    lengths,
+    adapters,
+    ranks,
+    slots,
+    x_hbm,
+    q_hbm,
+    k_hbm,
+    gain_hbm,
+    w_hbm,
+    down_hbm,
+    up_hbm,
+    out_hbm,
+    xs,
+    xf,
+    gain,
+    wbuf,
+    dn,
+    dcat,
+    up,
+    qb,
+    kb,
+    lp_mine,
+    lp_other,
+    part,
+    vr,
+    prob,
+    ob,
+    loc_sem,
+    x_send_up,
+    x_send_dn,
+    x_recv,
+    f_send,
+    f_recv,
+    w_send,
+    w_recv,
+    lp_send,
+    lp_recv,
+    q_send,
+    q_recv,
+    k_send,
+    k_recv,
+    rs_send,
+    rs_recv,
+    o_send,
+    o_recv,
+):
+    f32, bf16 = jnp.float32, jnp.bfloat16
+    s = lax.axis_index("seq")
+    o = lax.axis_index("owner")
+    tok, width = x_hbm.shape[1], x_hbm.shape[2]
+    half = width // 2
+    win = xf.shape[2]
+    slab = w_hbm.shape[1]
+    vcols = up.shape[2]
+    panel_count, _, rank_width = dn.shape
+    head_cols = vcols // n
+    q_cols = qb.shape[2]
+    group = HEADS // KEY_VALUE_HEADS
+    requests = lengths.shape[0]
+    total = n * tok
+    chip_rows = width // n
+    per_half = n // 2
+
+    def window(of):
+        inside = (of % per_half) * chip_rows
+        first = min(inside // LANES * LANES, half - win)
+        return first, inside - first
+
+    c = s // per_half
+    place = lax.rem(s, per_half)
+    first, pad = 0, 0
+    for step in range(per_half):
+        a, b = window(step)
+        first = jnp.where(place == step, a, first)
+        pad = jnp.where(place == step, b, pad)
+    first = pl.multiple_of(first, LANES)
+    other = 1 - o
+
+    def peer(seq, owner=None):
+        return {"seq": seq, "owner": o if owner is None else owner}
+
+    def remote(src, dst, send, recv, device):
+        return pltpu.make_async_remote_copy(
+            src_ref=src,
+            dst_ref=dst,
+            send_sem=send,
+            recv_sem=recv,
+            device_id=device,
+            device_id_type=pl.DeviceIdType.MESH,
+        )
+
+    for step in range(per_half):
+        _, b = window(step)
+
+        @pl.when(place == step)
+        def _():
+            if b:
+                wbuf[0:b, :] = jnp.zeros((b, vcols), bf16)
+            rest = win - b - chip_rows
+            if rest:
+                wbuf[win - rest : win, :] = jnp.zeros((rest, vcols), bf16)
+
+    barrier = pltpu.get_barrier_semaphore()
+    for d in range(1, n):
+        pl.semaphore_signal(
+            barrier, inc=1, device_id=peer(lax.rem(s + d, n)), device_id_type=pl.DeviceIdType.MESH
+        )
+    pl.semaphore_signal(barrier, inc=1, device_id=peer(s, other), device_id_type=pl.DeviceIdType.MESH)
+
+    w_at = pl.ds(pl.multiple_of(pad + o * slab, ROWS), slab)
+    my_cols = pl.ds(pl.multiple_of(o * vcols, LANES), vcols)
+    other_cols = pl.ds(pl.multiple_of(other * vcols, LANES), vcols)
+    my_half = pl.ds(pl.multiple_of(o * half, LANES), half)
+    x_window = pl.ds(pl.multiple_of(c * half + first, LANES), win)
+    my_head = pl.ds(pl.multiple_of(s * head_cols, LANES), head_cols)
+    my_q = pl.ds(pl.multiple_of(s * q_cols, LANES), q_cols)
+    local = [
+        pltpu.make_async_copy(x_hbm.at[0, :, my_half], xs.at[s], loc_sem.at[0]),
+        pltpu.make_async_copy(x_hbm.at[0, :, x_window], xf.at[s], loc_sem.at[1]),
+        pltpu.make_async_copy(gain_hbm, gain, loc_sem.at[2]),
+        pltpu.make_async_copy(down_hbm.at[0], dn, loc_sem.at[3]),
+        pltpu.make_async_copy(up_hbm.at[0], up, loc_sem.at[4]),
+        pltpu.make_async_copy(w_hbm.at[0, :, my_cols], wbuf.at[w_at], loc_sem.at[5]),
+        pltpu.make_async_copy(q_hbm.at[0, :, my_q], qb.at[s], loc_sem.at[6]),
+        pltpu.make_async_copy(k_hbm.at[0, :, my_head], kb.at[s], loc_sem.at[7]),
+    ]
+    for copy in local:
+        copy.start()
+
+    pl.semaphore_wait(barrier, n)
+
+    def x_copy(t, src, upward):
+        to = s + 1 if upward else s - 1
+        send = x_send_up if upward else x_send_dn
+        return remote(src, xs.at[t], send.at[t], x_recv.at[t], peer(to))
+
+    own_x = x_hbm.at[0, :, my_half]
+
+    @pl.when(s < n - 1)
+    def _():
+        x_copy(s, own_x, True).start()
+
+    @pl.when(s > 0)
+    def _():
+        x_copy(s, own_x, False).start()
+
+    w_copy = remote(w_hbm.at[0, :, other_cols], wbuf.at[w_at], w_send, w_recv, peer(s, other))
+    w_copy.start()
+
+    def q_copy(to):
+        cols = pl.ds(pl.multiple_of(to * q_cols, LANES), q_cols)
+        return remote(q_hbm.at[0, :, cols], qb.at[s], q_send.at[to], q_recv.at[s], peer(to))
+
+    def k_copy(to):
+        cols = pl.ds(pl.multiple_of(to * head_cols, LANES), head_cols)
+        return remote(k_hbm.at[0, :, cols], kb.at[s], k_send.at[to], k_recv.at[s], peer(to))
+
+    for d in range(1, n):
+        to = lax.rem(s + d, n)
+        q_copy(to).start()
+        k_copy(to).start()
+
+    ends, slot_of, rank_of = [], [], []
+    run = jnp.int32(0)
+    for r in range(requests):
+        run = run + lengths[r]
+        ends.append(run)
+        adapter = adapters[r]
+        slot_of.append(slots[adapter])
+        rank_of.append(ranks[adapter])
+
+    def request_at(position):
+        found = jnp.zeros(position.shape, jnp.int32)
+        for r in range(requests):
+            found = found + (position >= ends[r]).astype(jnp.int32)
+        return found
+
+    local[3].wait()
+    for p in range(panel_count):
+        dcat[:, p * rank_width : (p + 1) * rank_width] = dn[p]
+    for at in (0, 1, 2, 4, 5):
+        local[at].wait()
+
+    def f_copy(t):
+        return remote(
+            xs.at[t, :, pl.ds(first, win)], xf.at[t], f_send.at[t], f_recv.at[t], peer(s, other)
+        )
+
+    def lp_copy(t):
+        return remote(lp_mine.at[t], lp_other.at[t], lp_send.at[t], lp_recv.at[t], peer(s, other))
+
+    def rs_copy(t, to):
+        cols = pl.ds(pl.multiple_of(to * head_cols, LANES), head_cols)
+        return remote(part.at[t, :, cols], vr.at[s, t], rs_send.at[t, to], rs_recv.at[s, t], peer(to))
+
+    def low_part(t):
+        rows = xs[t].astype(f32)
+        scaled = (rows * gain[:, my_half]).astype(bf16)
+        square = jnp.sum(rows * rows, axis=1, keepdims=True)
+        product = jnp.dot(scaled, dcat[...], preferred_element_type=f32)
+        lp_mine[t, :, : panel_count * rank_width] = product
+        lp_mine[t, :, panel_count * rank_width :] = jnp.broadcast_to(square, (tok, LANES))
+        lp_copy(t).start()
+
+    def value_part(t):
+        scaled = (xf[t].astype(f32) * gain[:, x_window]).astype(bf16)
+        base = jnp.dot(scaled, wbuf[...], preferred_element_type=f32)
+        lp_copy(t).wait_recv()
+        low_width = panel_count * rank_width
+        square = lp_mine[t, :, low_width : low_width + 1] + lp_other[t, :, low_width : low_width + 1]
+        inv = lax.rsqrt(square / width + norm_eps)
+        low = (lp_mine[t, :, :low_width] + lp_other[t, :, :low_width]) * inv
+        req = request_at(t * tok + lax.broadcasted_iota(jnp.int32, (tok, 1), 0))
+        slot_t = jnp.zeros((tok, 1), jnp.int32)
+        rank_t = jnp.ones((tok, 1), jnp.int32)
+        for r in range(requests):
+            slot_t = jnp.where(req == r, slot_of[r], slot_t)
+            rank_t = jnp.where(req == r, rank_of[r], rank_t)
+        column = lax.broadcasted_iota(jnp.int32, (tok, low_width), 1)
+        begin = (slot_t - s * panel_count) * rank_width
+        low = jnp.where((column >= begin) & (column < begin + rank_t), low, 0.0).astype(bf16)
+        raised = jnp.dot(low, up[...].reshape(low_width, vcols), preferred_element_type=f32)
+        scale = adapter_strength / rank_t.astype(f32)
+        part[t] = (base * inv + raised * scale).astype(bf16)
+        for d in range(1, n):
+            rs_copy(t, lax.rem(s + d, n)).start()
+        vr[s, t] = part[t, :, my_head]
+
+    low_part(s)
+    w_copy.wait_recv()
+    value_part(s)
+
+    def attention():
+        local[6].wait()
+        local[7].wait()
+        for d in range(1, n):
+            frm = lax.rem(s + n - d, n)
+            remote(qb.at[frm], qb.at[frm], q_send.at[frm], q_recv.at[frm], peer(frm)).wait_recv()
+            remote(kb.at[frm], kb.at[frm], k_send.at[frm], k_recv.at[frm], peer(frm)).wait_recv()
+        keys = kb[...].reshape(total, head_cols)
+        key_at = lax.broadcasted_iota(jnp.int32, (1, total), 1)
+        key_req = request_at(key_at)
+        for t in range(n):
+            query_at = t * tok + lax.broadcasted_iota(jnp.int32, (tok, 1), 0)
+            live = (key_at <= query_at) & (key_at > query_at - WINDOW)
+            live = live & (request_at(query_at) == key_req)
+            for h in range(q_cols // HEAD_SIZE):
+                query = qb[t, :, h * HEAD_SIZE : (h + 1) * HEAD_SIZE]
+                kv = h // group
+                scores = (
+                    lax.dot_general(
+                        query,
+                        keys[:, kv * HEAD_SIZE : (kv + 1) * HEAD_SIZE],
+                        (((1,), (1,)), ((), ())),
+                        preferred_element_type=f32,
+                    )
+                    * query_scale
+                )
+                scores = jnp.where(live, scores, -1e30)
+                weights = jnp.exp(scores - jnp.max(scores, axis=1, keepdims=True))
+                soft = weights / jnp.sum(weights, axis=1, keepdims=True)
+                prob[h, t * tok : (t + 1) * tok, :] = soft.astype(bf16)
+
+    for d in range(1, n):
+        if d == n - 1:
+            attention()
+
+        def arrive(below):
+            t = s - d if below else s + d
+
+            @pl.when((t >= 0) if below else (t < n))
+            def _():
+                x_copy(t, xs.at[t], below).wait_recv()
+
+                @pl.when((s < n - 1) if below else (s > 0))
+                def _():
+                    x_copy(t, xs.at[t], below).start()
+
+                @pl.when(o == c)
+                def _():
+                    f_copy(t).start()
+                    xf[t] = xs[t, :, pl.ds(first, win)]
+
+        arrive(True)
+        arrive(False)
+
+        def both(side, carry):
+            t = s - d + 2 * d * side
+
+            @pl.when((t >= 0) & (t < n))
+            def _():
+                low_part(t)
+
+                @pl.when(o != c)
+                def _():
+                    f_copy(t).wait_recv()
+
+                value_part(t)
+
+            return carry
+
+        lax.fori_loop(0, 2, both, 0)
+
+    for d in range(1, n):
+        frm = lax.rem(s + d, n)
+        for t in range(n):
+            remote(vr.at[frm, t], vr.at[frm, t], rs_send.at[t, frm], rs_recv.at[frm, t], peer(frm)).wait_recv()
+    values = vr[0].astype(f32)
+    for frm in range(1, n):
+        values = values + vr[frm].astype(f32)
+    values = values.reshape(total, head_cols).astype(bf16)
+
+    def o_copy(t):
+        return remote(ob.at[t], out_hbm.at[0, :, my_q], o_send.at[t], o_recv.at[s], peer(t))
+
+    for h in range(q_cols // HEAD_SIZE):
+        kv = h // group
+        mixed = jnp.dot(
+            prob[h], values[:, kv * HEAD_SIZE : (kv + 1) * HEAD_SIZE], preferred_element_type=f32
+        ).astype(bf16)
+        ob[:, :, h * HEAD_SIZE : (h + 1) * HEAD_SIZE] = mixed.reshape(n, tok, HEAD_SIZE)
+    for d in range(1, n):
+        o_copy(lax.rem(s + d, n)).start()
+    mine = pltpu.make_async_copy(ob.at[s], out_hbm.at[0, :, my_q], loc_sem.at[8])
+    mine.start()
+
+    w_copy.wait_send()
+    for d in range(1, n):
+        to = lax.rem(s + d, n)
+        q_copy(to).wait_send()
+        k_copy(to).wait_send()
+        for t in range(n):
+            rs_copy(t, to).wait_send()
+    for t in range(n):
+        lp_copy(t).wait_send()
+
+        @pl.when((t <= s) & (s < n - 1))
+        def _():
+            x_copy(t, xs.at[t], True).wait_send()
+
+        @pl.when((t >= s) & (s > 0))
+        def _():
+            x_copy(t, xs.at[t], False).wait_send()
+
+        @pl.when((o == c) & (t != s))
+        def _():
+            f_copy(t).wait_send()
+
+    mine.wait()
+    for d in range(1, n):
+        frm = lax.rem(s + d, n)
+        o_copy(frm).wait_send()
+        cols = pl.ds(pl.multiple_of(frm * q_cols, LANES), q_cols)
+        remote(ob.at[frm], out_hbm.at[0, :, cols], o_send.at[frm], o_recv.at[frm], peer(frm)).wait_recv()
+
+
+def fused(
+    n,
+    layer_input_rows,
+    encoded_query_rows,
+    encoded_key_rows,
+    layer_norm_gain,
+    base_value_matrix,
+    adapter_down_panels,
+    adapter_up_panels,
+    request_token_lengths,
+    adapter_per_request,
+    rank_per_adapter,
+    slot_per_adapter,
+):
+    f32, bf16 = jnp.float32, jnp.bfloat16
+    tok, width = layer_input_rows.shape[1:]
+    half = width // 2
+    panels, _, rank_width = adapter_down_panels.shape[1:]
+    vcols = adapter_up_panels.shape[3]
+    qcols = encoded_query_rows.shape[2]
+    chip_rows = width // n
+    pads = [(i * chip_rows) % LANES for i in range(n // 2)]
+    win = -(-(max(pads) + chip_rows) // LANES) * LANES
+    total = n * tok
+    low = panels * rank_width
+    dma = pltpu.SemaphoreType.DMA
+    any_spec = pl.BlockSpec(memory_space=pl.ANY)
+    smem = pl.BlockSpec(memory_space=pltpu.SMEM)
+    return pl.pallas_call(
+        functools.partial(kernel, n),
+        out_shape=jax.ShapeDtypeStruct(encoded_query_rows.shape, bf16),
+        in_specs=[smem] * 4 + [any_spec] * 7,
+        out_specs=any_spec,
+        scratch_shapes=[
+            pltpu.VMEM((n, tok, half), bf16),
+            pltpu.VMEM((n, tok, win), bf16),
+            pltpu.VMEM((1, width), f32),
+            pltpu.VMEM((win, vcols), bf16),
+            pltpu.VMEM((panels, half, rank_width), bf16),
+            pltpu.VMEM((half, low), bf16),
+            pltpu.VMEM((panels, rank_width, vcols), bf16),
+            pltpu.VMEM((n, tok, qcols // n), bf16),
+            pltpu.VMEM((n, tok, vcols // n), bf16),
+            pltpu.VMEM((n, tok, low + LANES), f32),
+            pltpu.VMEM((n, tok, low + LANES), f32),
+            pltpu.VMEM((n, tok, vcols), bf16),
+            pltpu.VMEM((n, n, tok, vcols // n), bf16),
+            pltpu.VMEM((qcols // n // HEAD_SIZE, total, total), bf16),
+            pltpu.VMEM((n, tok, qcols // n), bf16),
+            dma((9,)),
+            dma((n,)),
+            dma((n,)),
+            dma((n,)),
+            dma((n,)),
+            dma((n,)),
+            dma,
+            dma,
+            dma((n,)),
+            dma((n,)),
+            dma((n,)),
+            dma((n,)),
+            dma((n,)),
+            dma((n,)),
+            dma((n, n)),
+            dma((n, n)),
+            dma((n,)),
+            dma((n,)),
+        ],
+        compiler_params=pltpu.CompilerParams(
+            collective_id=0, has_side_effects=True, vmem_limit_bytes=56 * 1024 * 1024
+        ),
+    )(
+        request_token_lengths,
+        adapter_per_request,
+        rank_per_adapter,
+        slot_per_adapter,
+        layer_input_rows,
+        encoded_query_rows,
+        encoded_key_rows,
+        layer_norm_gain,
+        base_value_matrix,
+        adapter_down_panels,
+        adapter_up_panels,
+    )
+
+
 def solution(mesh):
     in_specs = (
         P("segment", ("groups", "seq"), None),
@@ -164,6 +615,9 @@
         P(),
     )
     out_specs = P("segment", ("groups", "seq"), "owner")
+    n = mesh.shape["seq"]
+    key_heads = KEY_VALUE_HEADS // mesh.shape["owner"]
+    small = mesh.shape["owner"] == 2 and n % 2 == 0 and key_heads % n == 0
     return jax.shard_map(
-        per_device, mesh=mesh, in_specs=in_specs, out_specs=out_specs, check_vma=False
-    )
+        functools.partial(fused, n) if small else per_device, mesh=mesh, in_specs=in_specs, out_specs=out_specs, check_vma=False
+    )

time: 355 us -> 51.7 us (0.15)
  waiting for transfers between devices: 266 us -> 0 us
  Pallas kernels: 0 us -> 47.6 us
  loops' own time: 18.5 us -> 0 us
  matrix products: 15.6 us -> 0 us
  between operations: 14.9 us -> 0.01 us
  starting transfers between devices: 13.7 us -> 0 us
  other arithmetic: 10.8 us -> 0 us
  local copies, waits for them, and re-layouts: 11.6 us -> 3.96 us
    psum x4 -> x0, waiting for transfers between devices: 173 us -> none  [broadcast(): return lax.psum(jnp.where(mine, x, jnp.zeros_like(x)), axis)]
    all_gather x1 -> x0, waiting for transfers between devices: 90.8 us -> none  [per_device(): lax.all_gather(base_value_matrix[0], ('seq', 'owner'), axis=0, tiled=True)]
    pallas_call x0 -> x1, Pallas kernels: none -> 47.6 us  [fused(): pl.pallas_call(functools.partial(kernel, n), out_shape=jax.ShapeDtypeStru...]
    another operation x1 -> x0, loops' own time: 18.5 us -> none  [per_device(): lax.scan(fetch_one, start_low, jnp.arange(requests, dtype=jnp.int32))]
    dot_general x14 -> x0, matrix products: 14.3 us -> none  [the longest x1 6.14 us: per_device(): jnp.dot(normalized_rows, lax.all_gather(base_value_matrix[0], ('seq', 'ow...]
    ppermute x6 -> x0, starting transfers between devices: 13.5 us -> none  [from_behind(): lax.ppermute(value, axis, [(source, source + steps) for source in range(f...]
    dynamic_slice x9 -> x0, local copies, waits for them, and re-layouts: 4.73 us -> none  [the longest x4 2.35 us: per_device(): lax.scan(fetch_one, start_low, jnp.arange(requests, dtype=jnp.int32))]
    squeeze x4 -> x0, other arithmetic: 3.62 us -> none  [fetch_one(): down_piece[0]]
  transfers between devices with their start and end apart: 11 -> 0, of which waited for: 6 -> 0; matrix products, arithmetic and copies ran while one was open for 1% -> 0% of each run, Pallas kernels for 0% -> 0%
where the time goes in v1:
time: 51.7 us; the launch traced here: 51.5 us
  Pallas kernels  47.6 us (92%)
  local copies, waits for them, and re-layouts  3.96 us (8%)
    pallas_call x1, Pallas kernels, fused(): pl.pallas_call(functools.partial(kernel, n), out_shape=jax.ShapeDtypeStru...  47.6 us
    unnamed x2, local copies, waits for them, and re-layouts  3.96 us

profile of v1, /device:TPU:0, one launch (start us, length us, event | category | flops | bytes accessed | tf_op | source)
XLA Modules:
  0.0 51.5 jit_solution(1996898499345141019)
XLA Ops:
  0.0 2.4 %copy.12.down_hbm = bf16[1,2,2688,64]{3,2,1,0:T(8,128)(2,1)} copy(bf16[1,2,2688,64]{2,3,1,0:T(8,128)(2,1)} %param.16) | data formatting | bytes 1376256 | tf_op args[5]
  2.4 47.6 %shard_map.109 = bf16[1,64,1024]{2,1,0:T(8,128)(2,1)} custom-call(s32[4]{0:T(128)} %lengths.1, s32[4]{0:T(128)} %adapters.1, s32[8]{0:T(128)} %ranks.1, s32[8]{0:T(128)} %slots.1, bf16[1,64,5376]{2,1,0:T(8,128)(2,1)} %x_hbm.1, bf16[1,64,1024]{2,1,0:T(8,128)(2,1)} %q_hbm.1, bf16[1,64,512]{2,1,0:T(8,128)(2,1)} %k_hbm.1, f32[1,5376]{1,0:T(1,128)} %gain_hbm.1, ...), custom_call_target="tpu_custom_call" | custom-call | tf_op jit(solution)/shard_map/pallas_call | solution.py:545
  50.0 1.6 %copy.14 = bf16[1,64,1024]{2,1,0:T(8,128)(2,1)} copy(bf16[1,64,1024]{2,1,0:T(8,128)(2,1)} %shard_map.109) | data formatting | bytes 262144

commit v2 on v1

--- a/solution.py
+++ b/solution.py
@@ -175,7 +175,6 @@
     gain,
     wbuf,
     dn,
-    dcat,
     up,
     qb,
     kb,
@@ -212,7 +211,7 @@
     win = xf.shape[2]
     slab = w_hbm.shape[1]
     vcols = up.shape[2]
-    panel_count, _, rank_width = dn.shape
+    panel_count, rank_width, _ = dn.shape
     head_cols = vcols // n
     q_cols = qb.shape[2]
     group = HEADS // KEY_VALUE_HEADS
@@ -335,10 +334,7 @@
             found = found + (position >= ends[r]).astype(jnp.int32)
         return found
 
-    local[3].wait()
-    for p in range(panel_count):
-        dcat[:, p * rank_width : (p + 1) * rank_width] = dn[p]
-    for at in (0, 1, 2, 4, 5):
+    for at in range(6):
         local[at].wait()
 
     def f_copy(t):
@@ -357,7 +353,12 @@
         rows = xs[t].astype(f32)
         scaled = (rows * gain[:, my_half]).astype(bf16)
         square = jnp.sum(rows * rows, axis=1, keepdims=True)
-        product = jnp.dot(scaled, dcat[...], preferred_element_type=f32)
+        product = lax.dot_general(
+            scaled,
+            dn[...].reshape(panel_count * rank_width, half),
+            (((1,), (1,)), ((), ())),
+            preferred_element_type=f32,
+        )
         lp_mine[t, :, : panel_count * rank_width] = product
         lp_mine[t, :, panel_count * rank_width :] = jnp.broadcast_to(square, (tok, LANES))
         lp_copy(t).start()
@@ -387,8 +388,6 @@
         vr[s, t] = part[t, :, my_head]
 
     low_part(s)
-    w_copy.wait_recv()
-    value_part(s)
 
     def attention():
         local[6].wait()
@@ -443,6 +442,10 @@
 
         arrive(True)
         arrive(False)
+
+        if d == 1:
+            w_copy.wait_recv()
+            value_part(s)
 
         def both(side, carry):
             t = s - d + 2 * d * side
@@ -552,8 +555,7 @@
             pltpu.VMEM((n, tok, win), bf16),
             pltpu.VMEM((1, width), f32),
             pltpu.VMEM((win, vcols), bf16),
-            pltpu.VMEM((panels, half, rank_width), bf16),
-            pltpu.VMEM((half, low), bf16),
+            pltpu.VMEM((panels, rank_width, half), bf16),
             pltpu.VMEM((panels, rank_width, vcols), bf16),
             pltpu.VMEM((n, tok, qcols // n), bf16),
             pltpu.VMEM((n, tok, vcols // n), bf16),
@@ -595,7 +597,7 @@
         encoded_key_rows,
         layer_norm_gain,
         base_value_matrix,
-        adapter_down_panels,
+        jnp.swapaxes(adapter_down_panels, 2, 3),
         adapter_up_panels,
     )
 

time: 51.7 us -> 49.8 us (0.963)
  local copies, waits for them, and re-layouts: 3.96 us -> 1.57 us
    unnamed x2 -> x1, local copies, waits for them, and re-layouts: 3.96 us -> 1.57 us
    pallas_call x1, Pallas kernels: 47.6 us -> 48.1 us  [fused(): pl.pallas_call(functools.partial(kernel, n), out_shape=jax.ShapeDtypeStru...]
where the time goes in v2:
time: 49.8 us; the launch traced here: 49.7 us
  Pallas kernels  48.1 us (97%)
  local copies, waits for them, and re-layouts  1.57 us (3%)
    pallas_call x1, Pallas kernels, fused(): pl.pallas_call(functools.partial(kernel, n), out_shape=jax.ShapeDtypeStru...  48.1 us
    unnamed x1, local copies, waits for them, and re-layouts  1.57 us

profile of v2, /device:TPU:0, one launch (start us, length us, event | category | flops | bytes accessed | tf_op | source)
XLA Modules:
  0.0 49.7 jit_solution(15824318861563950945)
XLA Ops:
  0.0 48.1 %shard_map.109 = bf16[1,64,1024]{2,1,0:T(8,128)(2,1)} custom-call(s32[4]{0:T(128)} %lengths.1, s32[4]{0:T(128)} %adapters.1, s32[8]{0:T(128)} %ranks.1, s32[8]{0:T(128)} %slots.1, bf16[1,64,5376]{2,1,0:T(8,128)(2,1)} %x_hbm.1, bf16[1,64,1024]{2,1,0:T(8,128)(2,1)} %q_hbm.1, bf16[1,64,512]{2,1,0:T(8,128)(2,1)} %k_hbm.1, f32[1,5376]{1,0:T(1,128)} %gain_hbm.1, ...), custom_call_target="tpu_custom_call" | custom-call | tf_op jit(solution)/shard_map/pallas_call | solution.py:548
  48.1 1.6 %copy.13 = bf16[1,64,1024]{2,1,0:T(8,128)(2,1)} copy(bf16[1,64,1024]{2,1,0:T(8,128)(2,1)} %shard_map.109) | data formatting | bytes 262144

commit v3 on v2

--- a/solution.py
+++ b/solution.py
@@ -175,6 +175,9 @@
     gain,
     wbuf,
     dn,
+    dn_guest,
+    lp_host,
+    base,
     up,
     qb,
     kb,
@@ -202,6 +205,9 @@
     rs_recv,
     o_send,
     o_recv,
+    p_send,
+    p_recv,
+    hk_send,
 ):
     f32, bf16 = jnp.float32, jnp.bfloat16
     s = lax.axis_index("seq")
@@ -234,6 +240,15 @@
         pad = jnp.where(place == step, b, pad)
     first = pl.multiple_of(first, LANES)
     other = 1 - o
+    at_end = (s == 0) | (s == n - 1)
+    guest = at_end & (o != c)
+    keeper = at_end & (o == c)
+    host_low, host_high = (s == 1) & (o == 1), (s == n - 2) & (o == 0)
+    host = host_low | host_high
+    end_of_host = jnp.where(host_low, 0, n - 1)
+    host_seq = jnp.where(s == 0, 1, n - 2)
+    can_up = (s < n - 1) & jnp.logical_not(host_high)
+    can_down = (s > 0) & jnp.logical_not(host_low)
 
     def peer(seq, owner=None):
         return {"seq": seq, "owner": o if owner is None else owner}
@@ -265,6 +280,18 @@
             barrier, inc=1, device_id=peer(lax.rem(s + d, n)), device_id_type=pl.DeviceIdType.MESH
         )
     pl.semaphore_signal(barrier, inc=1, device_id=peer(s, other), device_id_type=pl.DeviceIdType.MESH)
+
+    @pl.when(host)
+    def _():
+        pl.semaphore_signal(
+            barrier, inc=1, device_id=peer(end_of_host, other), device_id_type=pl.DeviceIdType.MESH
+        )
+
+    @pl.when(keeper)
+    def _():
+        pl.semaphore_signal(
+            barrier, inc=1, device_id=peer(host_seq, other), device_id_type=pl.DeviceIdType.MESH
+        )
 
     w_at = pl.ds(pl.multiple_of(pad + o * slab, ROWS), slab)
     my_cols = pl.ds(pl.multiple_of(o * vcols, LANES), vcols)
@@ -286,7 +313,7 @@
     for copy in local:
         copy.start()
 
-    pl.semaphore_wait(barrier, n)
+    pl.semaphore_wait(barrier, n + (host | keeper).astype(jnp.int32))
 
     def x_copy(t, src, upward):
         to = s + 1 if upward else s - 1
@@ -295,13 +322,19 @@
 
     own_x = x_hbm.at[0, :, my_half]
 
-    @pl.when(s < n - 1)
+    @pl.when(can_up)
     def _():
         x_copy(s, own_x, True).start()
 
-    @pl.when(s > 0)
+    @pl.when(can_down)
     def _():
         x_copy(s, own_x, False).start()
+
+    panel_copy = remote(down_hbm.at[0], dn_guest, p_send, p_recv, peer(host_seq))
+
+    @pl.when(guest)
+    def _():
+        panel_copy.start()
 
     w_copy = remote(w_hbm.at[0, :, other_cols], wbuf.at[w_at], w_send, w_recv, peer(s, other))
     w_copy.start()
@@ -313,11 +346,6 @@
     def k_copy(to):
         cols = pl.ds(pl.multiple_of(to * head_cols, LANES), head_cols)
         return remote(k_hbm.at[0, :, cols], kb.at[s], k_send.at[to], k_recv.at[s], peer(to))
-
-    for d in range(1, n):
-        to = lax.rem(s + d, n)
-        q_copy(to).start()
-        k_copy(to).start()
 
     ends, slot_of, rank_of = [], [], []
     run = jnp.int32(0)
@@ -349,24 +377,52 @@
         cols = pl.ds(pl.multiple_of(to * head_cols, LANES), head_cols)
         return remote(part.at[t, :, cols], vr.at[s, t], rs_send.at[t, to], rs_recv.at[s, t], peer(to))
 
-    def low_part(t):
+    def host_copies(t):
+        return (
+            remote(lp_host.at[t], lp_other.at[t], hk_send.at[t], lp_recv.at[t], peer(end_of_host, other)),
+        )
+
+    def low_half(t, panels, result):
         rows = xs[t].astype(f32)
         scaled = (rows * gain[:, my_half]).astype(bf16)
         square = jnp.sum(rows * rows, axis=1, keepdims=True)
         product = lax.dot_general(
             scaled,
-            dn[...].reshape(panel_count * rank_width, half),
+            panels[...].reshape(panel_count * rank_width, half),
             (((1,), (1,)), ((), ())),
             preferred_element_type=f32,
         )
-        lp_mine[t, :, : panel_count * rank_width] = product
-        lp_mine[t, :, panel_count * rank_width :] = jnp.broadcast_to(square, (tok, LANES))
-        lp_copy(t).start()
+        result[t, :, : panel_count * rank_width] = product
+        result[t, :, panel_count * rank_width :] = jnp.broadcast_to(square, (tok, LANES))
+
+    @pl.when(guest)
+    def _():
+        lp_mine[...] = jnp.zeros(lp_mine.shape, f32)
+
+    def low_part(t):
+        @pl.when(jnp.logical_not(guest))
+        def _():
+            low_half(t, dn, lp_mine)
+
+        @pl.when(jnp.logical_not(at_end))
+        def _():
+            lp_copy(t).start()
+
+
+    def base_part(t):
+        scaled = (xf[t].astype(f32) * gain[:, x_window]).astype(bf16)
+        base[t] = jnp.dot(scaled, wbuf[...], preferred_element_type=f32)
 
     def value_part(t):
-        scaled = (xf[t].astype(f32) * gain[:, x_window]).astype(bf16)
-        base = jnp.dot(scaled, wbuf[...], preferred_element_type=f32)
         lp_copy(t).wait_recv()
+
+        @pl.when(keeper)
+        def _():
+            lp_host[t] = lp_mine[t] + lp_other[t]
+            remote(
+                lp_host.at[t], lp_other.at[t], lp_send.at[t], lp_recv.at[t], peer(s, other)
+            ).start()
+
         low_width = panel_count * rank_width
         square = lp_mine[t, :, low_width : low_width + 1] + lp_other[t, :, low_width : low_width + 1]
         inv = lax.rsqrt(square / width + norm_eps)
@@ -382,7 +438,7 @@
         low = jnp.where((column >= begin) & (column < begin + rank_t), low, 0.0).astype(bf16)
         raised = jnp.dot(low, up[...].reshape(low_width, vcols), preferred_element_type=f32)
         scale = adapter_strength / rank_t.astype(f32)
-        part[t] = (base * inv + raised * scale).astype(bf16)
+        part[t] = (base[t] * inv + raised * scale).astype(bf16)
         for d in range(1, n):
             rs_copy(t, lax.rem(s + d, n)).start()
         vr[s, t] = part[t, :, my_head]
@@ -422,16 +478,23 @@
 
     for d in range(1, n):
         if d == n - 1:
-            attention()
+
+            @pl.when(at_end)
+            def _():
+                def one(e, carry):
+                    value_part(jnp.where(s == 0, e, n - 1 - e))
+                    return carry
+
+                lax.fori_loop(0, n - 1, one, 0)
 
         def arrive(below):
             t = s - d if below else s + d
 
-            @pl.when((t >= 0) if below else (t < n))
+            @pl.when(((t >= 0) if below else (t < n)) & jnp.logical_not(guest))
             def _():
                 x_copy(t, xs.at[t], below).wait_recv()
 
-                @pl.when((s < n - 1) if below else (s > 0))
+                @pl.when(can_up if below else can_down)
                 def _():
                     x_copy(t, xs.at[t], below).start()
 
@@ -443,9 +506,33 @@
         arrive(True)
         arrive(False)
 
+        if d == n - 2:
+            for e in range(1, n):
+                to = lax.rem(s + e, n)
+                q_copy(to).start()
+                k_copy(to).start()
+
         if d == 1:
             w_copy.wait_recv()
-            value_part(s)
+            base_part(s)
+
+            @pl.when(jnp.logical_not(at_end))
+            def _():
+                value_part(s)
+
+        if d == n - 2:
+
+            @pl.when(host)
+            def _():
+                panel_copy.wait_recv()
+
+                def one(t, carry):
+                    low_half(t, dn_guest, lp_host)
+                    for copy in host_copies(t):
+                        copy.start()
+                    return carry
+
+                lax.fori_loop(0, n, one, 0)
 
         def both(side, carry):
             t = s - d + 2 * d * side
@@ -458,11 +545,17 @@
                 def _():
                     f_copy(t).wait_recv()
 
-                value_part(t)
+                base_part(t)
+
+                @pl.when(jnp.logical_not(at_end) | (d == n - 1))
+                def _():
+                    value_part(t)
 
             return carry
 
         lax.fori_loop(0, 2, both, 0)
+
+    attention()
 
     for d in range(1, n):
         frm = lax.rem(s + d, n)
@@ -488,6 +581,11 @@
     mine.start()
 
     w_copy.wait_send()
+
+    @pl.when(guest)
+    def _():
+        panel_copy.wait_send()
+
     for d in range(1, n):
         to = lax.rem(s + d, n)
         q_copy(to).wait_send()
@@ -495,13 +593,21 @@
         for t in range(n):
             rs_copy(t, to).wait_send()
     for t in range(n):
-        lp_copy(t).wait_send()
-
-        @pl.when((t <= s) & (s < n - 1))
+
+        @pl.when(jnp.logical_not(guest))
+        def _():
+            lp_copy(t).wait_send()
+
+        @pl.when(host)
+        def _():
+            for copy in host_copies(t):
+                copy.wait_send()
+
+        @pl.when((t <= s) & can_up)
         def _():
             x_copy(t, xs.at[t], True).wait_send()
 
-        @pl.when((t >= s) & (s > 0))
+        @pl.when((t >= s) & can_down)
         def _():
             x_copy(t, xs.at[t], False).wait_send()
 
@@ -556,6 +662,9 @@
             pltpu.VMEM((1, width), f32),
             pltpu.VMEM((win, vcols), bf16),
             pltpu.VMEM((panels, rank_width, half), bf16),
+            pltpu.VMEM((panels, rank_width, half), bf16),
+            pltpu.VMEM((n, tok, low + LANES), f32),
+            pltpu.VMEM((n, tok, vcols), f32),
             pltpu.VMEM((panels, rank_width, vcols), bf16),
             pltpu.VMEM((n, tok, qcols // n), bf16),
             pltpu.VMEM((n, tok, vcols // n), bf16),
@@ -582,6 +691,9 @@
             dma((n, n)),
             dma((n, n)),
             dma((n,)),
+            dma((n,)),
+            dma,
+            dma,
             dma((n,)),
         ],
         compiler_params=pltpu.CompilerParams(
@@ -619,7 +731,7 @@
     out_specs = P("segment", ("groups", "seq"), "owner")
     n = mesh.shape["seq"]
     key_heads = KEY_VALUE_HEADS // mesh.shape["owner"]
-    small = mesh.shape["owner"] == 2 and n % 2 == 0 and key_heads % n == 0
+    small = mesh.shape["owner"] == 2 and n % 4 == 0 and key_heads % n == 0
     return jax.shard_map(
         functools.partial(fused, n) if small else per_device, mesh=mesh, in_specs=in_specs, out_specs=out_specs, check_vma=False
     )

time: 49.8 us -> 47.3 us (0.950)
  Pallas kernels: 48.1 us -> 45.6 us
    pallas_call x1, Pallas kernels: 48.1 us -> 45.6 us  [fused(): pl.pallas_call(functools.partial(kernel, n), out_shape=jax.ShapeDtypeStru...]
where the time goes in v3:
time: 47.3 us; the launch traced here: 47.2 us
  Pallas kernels  45.6 us (96%)
  local copies, waits for them, and re-layouts  1.57 us (3%)
    pallas_call x1, Pallas kernels, fused(): pl.pallas_call(functools.partial(kernel, n), out_shape=jax.ShapeDtypeStru...  45.6 us
    unnamed x1, local copies, waits for them, and re-layouts  1.57 us

profile of v3, /device:TPU:0, one launch (start us, length us, event | category | flops | bytes accessed | tf_op | source)
XLA Modules:
  0.0 47.2 jit_solution(12749461980333589224)
XLA Ops:
  0.0 45.6 %shard_map.109 = bf16[1,64,1024]{2,1,0:T(8,128)(2,1)} custom-call(s32[4]{0:T(128)} %lengths.1, s32[4]{0:T(128)} %adapters.1, s32[8]{0:T(128)} %ranks.1, s32[8]{0:T(128)} %slots.1, bf16[1,64,5376]{2,1,0:T(8,128)(2,1)} %x_hbm.1, bf16[1,64,1024]{2,1,0:T(8,128)(2,1)} %q_hbm.1, bf16[1,64,512]{2,1,0:T(8,128)(2,1)} %k_hbm.1, f32[1,5376]{1,0:T(1,128)} %gain_hbm.1, ...), custom_call_target="tpu_custom_call" | custom-call | tf_op jit(solution)/shard_map/pallas_call | solution.py:654
  45.6 1.6 %copy.13 = bf16[1,64,1024]{2,1,0:T(8,128)(2,1)} copy(bf16[1,64,1024]{2,1,0:T(8,128)(2,1)} %shard_map.109) | data formatting | bytes 262144
